TPU v7x, 256 devices: a whole 4x4x8 slice. The times are simulated.
256 devices in a mesh: dp: 16 (over y, x), seq: 16 (over z, core).
Axes of the slice: x: 4, y: 4, z: 8, core: 2. Of those that a mesh axis runs over, the one named last changes fastest.
Arguments:
- query_proj: bfloat16 [16, 3072, 1024], P('dp', 'seq'), may hold values from -6 to 6
- key_proj: bfloat16 [16, 3072, 1024], P('dp', 'seq'), may hold values from -6 to 6
- value_proj: bfloat16 [16, 3072, 1024], P('dp', 'seq'), may hold values from -6 to 6
- cotangent: bfloat16 [16, 3072, 1024], P('dp', 'seq'), may hold values from -6 to 6
- out_weight: bfloat16 [1024, 1024], replicated, may hold values from -0.1875 to 0.1875
- conv_weight: float32 [31, 1024], replicated, may hold values from -1 to 1
- rec_starts: int32 [16, 2], P('dp'), may hold values from 0 to 3064, as said below
Outputs:
- layer_out: bfloat16 [16, 3072, 1024], P('dp', 'seq')
- query_grad: bfloat16 [16, 3072, 1024], P('dp', 'seq')
- key_grad: bfloat16 [16, 3072, 1024], P('dp', 'seq')
- value_grad: bfloat16 [16, 3072, 1024], P('dp', 'seq')
- weight_grad: float32 [1024, 1024], replicated
- conv_grad: float32 [31, 1024], replicated
Inputs may be any that keep to these rules, and one draw needn't show every extreme that they name: `rec_starts`: in each group the first start is 0, the starts rise strictly and each is a multiple of 8; a recording runs up to the next start, the last one to frame 3072 - 1.
All inputs are finite; a program needn't handle non-finite values.
Results may differ from a plain program's by a relative error of at most 0.02.
Values may be sent and summed in bfloat16 or wider, within the bound.
A program may use at most 64 MiB of HBM per device.

v0:
```python
import math
import jax
import jax.numpy as jnp
from jax import lax
from jax.sharding import PartitionSpec as P

HEAD_DIM = 64
KERN = 31
LAG = 30


def shifted(value, axis, steps):
    count = lax.axis_size(axis)
    leading, last = (max(0, -steps), min(count, count - steps))
    return lax.ppermute(value, axis, [(source, source + steps) for source in range(leading, last)])


def record_ids(frames, starts_row, total):
    above = (frames[:, None] >= starts_row[None, :]).astype(jnp.int32)
    labels = jnp.sum(above, axis=1) - 1
    inside = (frames >= 0) & (frames < total)
    return jnp.where(inside, labels, -2)


def depthwise(padded, labels_pad, labels_out, weights, count):
    total = jnp.zeros((count, padded.shape[1]), jnp.float32)
    for tap in range(weights.shape[0]):
        window = padded[tap : tap + count].astype(jnp.float32)
        same = (labels_pad[tap : tap + count] == labels_out)[:, None]
        total = total + jnp.where(same, weights[tap][None, :] * window, 0.0)
    return total


def transposed(padded, labels_pad, labels_out, weights, count):
    total = jnp.zeros((count, padded.shape[1]), jnp.float32)
    last = weights.shape[0] - 1
    for tap in range(weights.shape[0]):
        offset = last - tap
        window = padded[offset : offset + count].astype(jnp.float32)
        same = (labels_pad[offset : offset + count] == labels_out)[:, None]
        total = total + jnp.where(same, weights[tap][None, :] * window, 0.0)
    return total


def tap_sums(signal, padded, labels_pad, labels_out, taps):
    count = signal.shape[0]
    rows_out = []
    for tap in range(taps):
        window = padded[tap : tap + count].astype(jnp.float32)
        same = (labels_pad[tap : tap + count] == labels_out)[:, None]
        rows_out.append(jnp.sum(jnp.where(same, signal * window, 0.0), axis=0))
    return jnp.stack(rows_out)


def silu_parts(conv):
    gate_value = jax.nn.sigmoid(conv)
    return (conv * gate_value, gate_value * (1.0 + conv * (1.0 - gate_value)))


def block_scores(query_blk, key_part, labels_q, labels_k, scale):
    raw = (
        jnp.einsum("qhd,khd->hqk", query_blk, key_part, preferred_element_type=jnp.float32) * scale
    )
    same = (labels_q[:, None] == labels_k[None, :])[None]
    return jnp.where(same, raw, -1e30)


def block_grads(
    query_blk, key_part, value_part, mixed_blk, back_blk, labels_q, labels_k, norm_blk, scale
):
    scores = block_scores(query_blk, key_part, labels_q, labels_k, scale)
    probs = jnp.exp(scores - norm_blk[:, :, None]).astype(jnp.bfloat16)
    prob_back = jnp.einsum("qhd,khd->hqk", back_blk, value_part, preferred_element_type=jnp.float32)
    delta = jnp.sum(back_blk.astype(jnp.float32) * mixed_blk.astype(jnp.float32), axis=2).T
    score_back = (probs.astype(jnp.float32) * (prob_back - delta[:, :, None])).astype(jnp.bfloat16)
    return (probs, score_back)


def forward_dense(heads_q, heads_k, heads_v, labels, width, scale):
    total, heads_here, features = heads_q.shape
    count = total // width

    def forward_one_block(index):
        start = index * width
        query_blk = lax.dynamic_slice_in_dim(heads_q, start, width, 0)
        labels_q = lax.dynamic_slice_in_dim(labels, start, width, 0)
        scores = block_scores(query_blk, heads_k, labels_q, labels, scale)
        top = jnp.max(scores, axis=2, keepdims=True)
        norm = top + jnp.log(jnp.sum(jnp.exp(scores - top), axis=2, keepdims=True))
        probs = jnp.exp(scores - norm).astype(jnp.bfloat16)
        mixed_blk = jnp.einsum("hqk,khd->qhd", probs, heads_v, preferred_element_type=jnp.float32)
        return (mixed_blk.astype(jnp.bfloat16), norm[:, :, 0])

    mixed_blocks, norm_blocks = lax.map(forward_one_block, jnp.arange(count, dtype=jnp.int32))
    mixed_heads = mixed_blocks.reshape(total, heads_here, features)
    norms = norm_blocks.transpose(1, 0, 2).reshape(heads_here, total)
    return (mixed_heads, norms)


def backward_dense(heads_q, heads_k, heads_v, mixed_heads, back_heads, norms, labels, width, scale):
    total = heads_q.shape[0]
    count = total // width
    empty = jnp.zeros(heads_k.shape, jnp.float32)

    def backward_one_block(carry, index):
        key_acc, value_acc = carry
        start = index * width
        query_blk = lax.dynamic_slice_in_dim(heads_q, start, width, 0)
        mixed_blk = lax.dynamic_slice_in_dim(mixed_heads, start, width, 0)
        back_blk = lax.dynamic_slice_in_dim(back_heads, start, width, 0)
        labels_q = lax.dynamic_slice_in_dim(labels, start, width, 0)
        norm_blk = lax.dynamic_slice_in_dim(norms, start, width, 1)
        probs, score_back = block_grads(
            query_blk, heads_k, heads_v, mixed_blk, back_blk, labels_q, labels, norm_blk, scale
        )
        query_part = scale * jnp.einsum(
            "hqk,khd->qhd", score_back, heads_k, preferred_element_type=jnp.float32
        )
        key_acc = key_acc + scale * jnp.einsum(
            "hqk,qhd->khd", score_back, query_blk, preferred_element_type=jnp.float32
        )
        value_acc = value_acc + jnp.einsum(
            "hqk,qhd->khd", probs, back_blk, preferred_element_type=jnp.float32
        )
        return ((key_acc, value_acc), query_part.astype(jnp.bfloat16))

    sums, query_blocks = lax.scan(
        backward_one_block, (empty, empty), jnp.arange(count, dtype=jnp.int32)
    )
    query_grads = query_blocks.reshape(heads_q.shape)
    return (query_grads, sums[0].astype(jnp.bfloat16), sums[1].astype(jnp.bfloat16))


def local(query_proj, key_proj, value_proj, cotangent, out_weight, conv_weight, rec_starts):
    rows = query_proj.shape[1]
    parts = lax.axis_size("seq")
    place = lax.axis_index("seq")
    total = rows * parts
    width = min(512, total)
    scale = HEAD_DIM ** (-0.5)
    starts_row = rec_starts[0]
    sent = (
        lax.all_to_all(query_proj[0], "seq", split_axis=1, concat_axis=0, tiled=True),
        lax.all_to_all(key_proj[0], "seq", split_axis=1, concat_axis=0, tiled=True),
        lax.all_to_all(value_proj[0], "seq", split_axis=1, concat_axis=0, tiled=True),
    )
    heads_q = sent[0].reshape(total, -1, HEAD_DIM)
    heads_k = sent[1].reshape(total, -1, HEAD_DIM)
    heads_v = sent[2].reshape(total, -1, HEAD_DIM)
    labels = record_ids(jnp.arange(total, dtype=jnp.int32), starts_row, total)
    mixed_heads, norms = forward_dense(heads_q, heads_k, heads_v, labels, width, scale)
    mixed_rows = lax.all_to_all(
        mixed_heads.reshape(total, -1), "seq", split_axis=0, concat_axis=1, tiled=True
    )
    projected = jnp.dot(mixed_rows, out_weight, preferred_element_type=jnp.float32).astype(
        jnp.bfloat16
    )
    labels_local = record_ids(place * rows + jnp.arange(rows, dtype=jnp.int32), starts_row, total)
    cot = cotangent[0]
    behind = shifted(projected[rows - LAG :], "seq", 1)
    padded = jnp.concatenate([behind, projected], axis=0)
    labels_pad = record_ids(
        place * rows - LAG + jnp.arange(rows + LAG, dtype=jnp.int32), starts_row, total
    )
    labels_back = record_ids(
        place * rows + jnp.arange(rows + LAG, dtype=jnp.int32), starts_row, total
    )
    conv = depthwise(padded, labels_pad, labels_local, conv_weight, rows)
    activated, slope = silu_parts(conv)
    conv_back = cot.astype(jnp.float32) * slope
    ahead_back = shifted(conv_back[:LAG].astype(jnp.bfloat16), "seq", -1).astype(jnp.float32)
    back_pad = jnp.concatenate([conv_back, ahead_back], axis=0)
    layer_out = (projected.astype(jnp.float32) + activated).astype(jnp.bfloat16)
    spread = transposed(back_pad, labels_back, labels_local, conv_weight, rows)
    proj_back = (cot.astype(jnp.float32) + spread).astype(jnp.bfloat16)
    conv_local = tap_sums(conv_back, padded, labels_pad, labels_local, KERN)
    factor = 1.0 / math.sqrt(lax.axis_size("dp") * total)
    weight_local = lax.dot_general(
        mixed_rows, proj_back, (((0,), (0,)), ((), ())), preferred_element_type=jnp.float32
    )
    summed = lax.psum((weight_local, conv_local), ("dp", "seq"))
    weight_grad = summed[0] * factor
    conv_grad = summed[1] * factor
    mixed_back = lax.dot_general(
        proj_back, out_weight, (((1,), (1,)), ((), ())), preferred_element_type=jnp.float32
    ).astype(jnp.bfloat16)
    back_heads = lax.all_to_all(mixed_back, "seq", split_axis=1, concat_axis=0, tiled=True).reshape(
        total, -1, HEAD_DIM
    )
    grad_q, grad_k, grad_v = backward_dense(
        heads_q, heads_k, heads_v, mixed_heads, back_heads, norms, labels, width, scale
    )
    returned = (
        lax.all_to_all(grad_q.reshape(total, -1), "seq", split_axis=0, concat_axis=1, tiled=True),
        lax.all_to_all(grad_k.reshape(total, -1), "seq", split_axis=0, concat_axis=1, tiled=True),
        lax.all_to_all(grad_v.reshape(total, -1), "seq", split_axis=0, concat_axis=1, tiled=True),
    )
    return (
        layer_out[None],
        returned[0][None],
        returned[1][None],
        returned[2][None],
        weight_grad,
        conv_grad,
    )


def solution(mesh):
    return jax.shard_map(
        local,
        mesh=mesh,
        in_specs=(
            P("dp", "seq", None),
            P("dp", "seq", None),
            P("dp", "seq", None),
            P("dp", "seq", None),
            P(),
            P(),
            P("dp", None),
        ),
        out_specs=(
            P("dp", "seq", None),
            P("dp", "seq", None),
            P("dp", "seq", None),
            P("dp", "seq", None),
            P(),
            P(),
        ),
        check_vma=False,
    )
```

profile of v0, /device:TPU:2, one launch (start us, length us, event | category | flops | bytes accessed | tf_op | source)
XLA Modules:
  0.0 611.4 jit_solution(17486042419321726274)
XLA Ops:
  7.2 2.1 copy.56
  9.3 8.6 %all-to-all-start = ((bf16[192,16,64]{0,2,1:T(8,128)(2,1)}), bf16[192,16,64]{0,2,1:T(8,128)(2,1)S(1)}, u32[]{:S(2)}, u32[]{:S(2)}) async-start(bf16[192,16,64]{0,2,1:T(8,128)(2,1)} %bitcast.10), calls=%async_computation | async-start | bytes 1048576 | tf_op jit(solution)/shard_map/all_to_all | solution.py:143
  17.9 2.0 copy.58
  19.9 2.0 copy.60
  21.9 12.0 %all-to-all-done = bf16[192,16,64]{0,2,1:T(8,128)(2,1)S(1)} async-done(((bf16[192,16,64]{0,2,1:T(8,128)(2,1)}), bf16[192,16,64]{0,2,1:T(8,128)(2,1)S(1)}, u32[]{:S(2)}, u32[]{:S(2)}) %all-to-all-start) | async-done | bytes 393248 | tf_op jit(solution)/shard_map/all_to_all | solution.py:143
  33.9 4.2 all-to-all-start.1
  39.7 14.6 %all-to-all-done.1 = bf16[192,16,64]{0,2,1:T(8,128)(2,1)S(1)} async-done(((bf16[192,16,64]{0,2,1:T(8,128)(2,1)}), bf16[192,16,64]{0,2,1:T(8,128)(2,1)S(1)}, u32[]{:S(2)}, u32[]{:S(2)}) %all-to-all-start.1) | async-done | bytes 393248 | tf_op jit(solution)/shard_map/all_to_all | solution.py:144
  54.3 4.2 all-to-all-start.2
  64.1 10.5 %all-to-all-done.2 = bf16[192,16,64]{0,2,1:T(8,128)(2,1)} async-done(((bf16[192,16,64]{0,2,1:T(8,128)(2,1)}), bf16[192,16,64]{0,2,1:T(8,128)(2,1)}, u32[]{:S(2)}, u32[]{:S(2)}) %all-to-all-start.2) | async-done | bytes 393248 | tf_op jit(solution)/shard_map/all_to_all | solution.py:145
  76.5 37.1 %while.27 = (s32[]{:T(128)}, bf16[6,512,1,64]{1,3,2,0:T(8,128)(2,1)S(1)}, f32[6,1,512]{2,1,0:T(1,128)}, s32[6]{0:T(128)S(1)}, s32[3072]{0:T(1024)S(1)}, /*index=...) while((s32[]{:T(128)}, ...), condition=%wide.region_4.5_spmd, body=%wide.region_1.4_spmd.sunk | while | flops 415268352 | bytes 19828936 | solution.py:94
  77.9 2.1 fusion.340
  84.1 2.1 fusion.340
  90.2 2.1 fusion.340
  96.4 2.1 fusion.340
  102.6 2.1 fusion.340
  108.8 2.1 fusion.340
  114.7 2.5 all_to_all.107
  117.2 2.0 copy.63
  119.2 4.1 all-to-all-start.3
  124.7 1.7 fusion.312
  126.4 2.0 fusion.311
  128.5 11.0 %all-to-all-done.3 = bf16[16,192,64]{1,2,0:T(8,128)(2,1)S(1)} async-done(((bf16[16,192,64]{1,2,0:T(8,128)(2,1)}), bf16[16,192,64]{1,2,0:T(8,128)(2,1)S(1)}, u32[]{:S(2)}, u32[]{:S(2)}) %all-to-all-start.3) | async-done | bytes 393248 | tf_op jit(solution)/shard_map/all_to_all | solution.py:152
  140.8 3.6 collective-permute-start
  146.2 1.9 copy.74
  148.1 19.4 %fusion.155 = (f32[1024]{0:T(1024)S(1)}, f32[192,1024]{1,0:T(8,128)S(1)}, f32[192,1024]{1,0:T(8,128)}) fusion(bf16[192,1024]{1,0:T(8,128)(2,1)} %copy-done.1, pred[192]{0:T(512)(128)(4,1)} %get-tuple-element.318, bf16[1,192,1024]{2,1,0:T(8,128)(2,1)} %param.14, f32[1024]{0:T(1024)} %bitcast.257, bf16[30,1024]{1,0:T(8,128)(2,1)S(1)} %collective-permute-done, ...), kind=kLoop, calls=%fused_computation.322 | loop fusion | flops 44235776 | bytes 2557760 | tf_op jit(solution)/shard_map/reduce_sum | solution.py:51
  168.8 3.9 fusion.90
  172.8 4.0 fusion.108
  176.8 2.7 fusion.72
  179.8 9.1 %fusion.151 = bf16[192,1024]{1,0:T(8,128)(2,1)S(1)} fusion(f32[192,1024]{1,0:T(8,128)S(1)} %get-tuple-element.250, f32[30,1024]{1,0:T(8,128)S(1)} %convert_element_type.251, bf16[1,192,1024]{2,1,0:T(8,128)(2,1)S(1)} %copy-done.15, f32[1024]{0:T(1024)S(1)} %bitcast.258, f32[1024]{0:T(1024)S(1)} %bitcast.260, f32[1024]{0:T(1024)S(1)} %bitcast.264, ...), kind=kLoop, calls=%fused_computation.318 | loop fusion | flops 24576000 | bytes 1828672 | tf_op jit(solution)/shard_map/convert_element_type | solution.py:175
  191.4 2.0 copy.64
  193.4 6.2 %all-to-all-start.4 = ((bf16[192,16,64]{0,2,1:T(8,128)(2,1)}), bf16[192,16,64]{0,2,1:T(8,128)(2,1)}, u32[]{:S(2)}, u32[]{:S(2)}) async-start(bf16[192,16,64]{0,2,1:T(8,128)(2,1)} %bitcast.230), calls=%async_computation.4 | async-start | bytes 1048576 | tf_op jit(solution)/shard_map/all_to_all | solution.py:187
  199.5 4.1 fusion.150
  203.7 4.2 fusion.126
  207.9 2.7 stack.127
  210.5 5.1 all-to-all-done.4
  219.0 82.6 %while.28 = (s32[]{:T(128)}, f32[3072,1,64]{0,2,1:T(8,128)}, f32[3072,1,64]{0,2,1:T(8,128)}, bf16[6,512,1,64]{1,3,2,0:T(8,128)(2,1)}, s32[6]{0:T(128)S(1)}, /*in...) while((s32[]{:T(128)}, f32[3072,1,64]{0,2,1:T(8,128)}, ...), condition=%wide.region_10.11_spmd.clone, body=%wide.region_8.10_spmd.clone.sunk | while | flops 1021967872 | bytes 37843340 | solution.py:127
  222.1 2.7 exponential_convert_fusion.12
  226.5 2.0 multiply_convert_fusion.2
  228.6 1.7 fusion.354
  235.8 2.8 exponential_convert_fusion.12
  240.3 2.0 multiply_convert_fusion.2
  249.6 2.7 exponential_convert_fusion.12
  254.0 2.0 multiply_convert_fusion.2
  263.3 2.7 exponential_convert_fusion.12
  267.8 2.0 multiply_convert_fusion.2
  277.1 2.8 exponential_convert_fusion.12
  281.6 2.0 multiply_convert_fusion.2
  290.9 2.7 exponential_convert_fusion.12
  295.3 2.0 multiply_convert_fusion.2
  304.4 4.2 all-to-all-start.5
  308.7 3.9 fusion.313
  312.7 2.0 convert_element_type.254
  314.6 2.4 all_to_all.117
  317.1 2.0 copy.69
  319.1 5.8 all-to-all-done.5
  324.8 4.2 all-to-all-start.6
  332.5 15.0 %all-to-all-done.6 = bf16[16,192,64]{1,2,0:T(8,128)(2,1)} async-done(((bf16[16,192,64]{1,2,0:T(8,128)(2,1)}), bf16[16,192,64]{1,2,0:T(8,128)(2,1)}, u32[]{:S(2)}, u32[]{:S(2)}) %all-to-all-start.6) | async-done | bytes 393248 | tf_op jit(solution)/shard_map/all_to_all | solution.py:195
  347.5 3.8 all-to-all-start.7
  351.3 2.1 fusion.304
  353.5 2.0 copy.71
  355.5 2.0 copy.72
  357.4 11.8 %all-to-all-done.7 = bf16[16,192,64]{1,2,0:T(8,128)(2,1)S(1)} async-done(((bf16[16,192,64]{1,2,0:T(8,128)(2,1)}), bf16[16,192,64]{1,2,0:T(8,128)(2,1)S(1)}, u32[]{:S(2)}, u32[]{:S(2)}) %all-to-all-start.7) | async-done | bytes 393248 | tf_op jit(solution)/shard_map/all_to_all | solution.py:196
  370.2 228.6 %all-reduce.3.cloned.1.call-done = (f32[1024,1024]{1,0:T(8,128)}, f32[31,1024]{1,0:T(8,128)}) async-done(((f32[1024,1024]{1,0:T(8,128)}, f32[31,1024]{1,0:T(8,128)}), (f32[1024,1024]{1,0:T(8,128)}, f32[31,1024]{1,0:T(8,128)})) %all-reduce.3.cloned.1.call-update) | async-done | bytes 4321296 | tf_op jit(solution)/shard_map/psum | solution.py:181
  598.8 5.2 broadcast_multiply_fusion
  (292 shorter events, 97.5 us)
Async XLA Ops:
  7.2 132.3 %copy-start = (bf16[1024,1024]{1,0:T(8,128)(2,1)S(1)}, bf16[1024,1024]{1,0:T(8,128)(2,1)}, u32[]{:S(2)}) copy-start(bf16[1024,1024]{1,0:T(8,128)(2,1)} %param.15) | copy-start | bytes 6291460
  9.3 24.6 %all-to-all-start = ((bf16[192,16,64]{0,2,1:T(8,128)(2,1)}), bf16[192,16,64]{0,2,1:T(8,128)(2,1)S(1)}, u32[]{:S(2)}, u32[]{:S(2)}) async-start(bf16[192,16,64]{0,2,1:T(8,128)(2,1)} %bitcast.10), calls=%async_computation | async-start | bytes 1048576 | tf_op jit(solution)/shard_map/all_to_all | solution.py:143
  33.9 20.4 %all-to-all-start.1 = ((bf16[192,16,64]{0,2,1:T(8,128)(2,1)}), bf16[192,16,64]{0,2,1:T(8,128)(2,1)S(1)}, u32[]{:S(2)}, u32[]{:S(2)}) async-start(bf16[192,16,64]{0,2,1:T(8,128)(2,1)} %bitcast.12), calls=%async_computation.1 | async-start | bytes 1048576 | tf_op jit(solution)/shard_map/all_to_all | solution.py:144
  54.3 6.3 %copy-start.14 = (bf16[192,16,64]{0,2,1:T(8,128)(2,1)}, bf16[192,16,64]{0,2,1:T(8,128)(2,1)S(1)}, u32[]{:S(2)}) copy-start(bf16[192,16,64]{0,2,1:T(8,128)(2,1)S(1)} %all-to-all-done.1) | copy-start | bytes 1179652
  54.3 20.3 %all-to-all-start.2 = ((bf16[192,16,64]{0,2,1:T(8,128)(2,1)}), bf16[192,16,64]{0,2,1:T(8,128)(2,1)}, u32[]{:S(2)}, u32[]{:S(2)}) async-start(bf16[192,16,64]{0,2,1:T(8,128)(2,1)} %bitcast.14), calls=%async_computation.2 | async-start | bytes 1048576 | tf_op jit(solution)/shard_map/all_to_all | solution.py:145
  59.9 64.1 %copy-start.48 = (s32[192]{0:T(256)}, s32[192]{0:T(256)S(1)}, u32[]{:S(2)}) copy-start(s32[192]{0:T(256)S(1)} %get-tuple-element.253) | copy-start | bytes 2308
  113.6 34.4 %copy-start.9 = (bf16[3072,1,64]{0,2,1:T(8,128)(2,1)}, bf16[3072,1,64]{0,2,1:T(8,128)(2,1)S(1)}, u32[]{:S(2)}) copy-start(bf16[3072,1,64]{0,2,1:T(8,128)(2,1)S(1)} %get-tuple-element.567) | copy-start | bytes 1179652
  119.2 20.3 %all-to-all-start.3 = ((bf16[16,192,64]{1,2,0:T(8,128)(2,1)}), bf16[16,192,64]{1,2,0:T(8,128)(2,1)S(1)}, u32[]{:S(2)}, u32[]{:S(2)}) async-start(bf16[16,192,64]{1,2,0:T(8,128)(2,1)} %copy.63), calls=%async_computation.3 | async-start | bytes 1048576 | tf_op jit(solution)/shard_map/all_to_all | solution.py:152
  139.4 8.6 %copy-start.11 = (bf16[16,192,64]{1,2,0:T(8,128)(2,1)}, bf16[16,192,64]{1,2,0:T(8,128)(2,1)S(1)}, u32[]{:S(2)}) copy-start(bf16[16,192,64]{1,2,0:T(8,128)(2,1)S(1)} %all-to-all-done.3) | copy-start | bytes 1179652
  140.8 7.2 %collective-permute-start = (bf16[30,1024]{1,0:T(8,128)(2,1)S(1)}, bf16[30,1024]{1,0:T(8,128)(2,1)S(1)}, u32[]{:S(2)}, u32[]{:S(2)}) collective-permute-start(bf16[30,1024]{1,0:T(8,128)(2,1)S(1)} %slice.713), channel_id=1, source_target_pairs={{0,1},{1,2},{2,3},{3,4},{4,5},{5,6},{6,7},{7,8},{8,9},{9,10},{10,1... | collective-permute-start | bytes 184328 | tf_op jit(solution)/shard_map/ppermute | solution.py:15
  145.8 33.7 %copy-start.17 = (f32[1,1024]{1,0:T(1,128)S(1)}, f32[1,1024]{1,0:T(1,128)}, u32[]{:S(2)}) copy-start(f32[1,1024]{1,0:T(1,128)} %get-tuple-element.275) | copy-start | bytes 12292
  145.8 30.9 %copy-start.2 = (bf16[192,1024]{1,0:T(8,128)(2,1)S(1)}, bf16[192,1024]{1,0:T(8,128)(2,1)}, u32[]{:S(2)}) copy-start(bf16[192,1024]{1,0:T(8,128)(2,1)} %copy-done.1) | copy-start | bytes 1179652
  145.8 33.6 %copy-start.15 = (bf16[1,192,1024]{2,1,0:T(8,128)(2,1)S(1)}, bf16[1,192,1024]{2,1,0:T(8,128)(2,1)}, u32[]{:S(2)}) copy-start(bf16[1,192,1024]{2,1,0:T(8,128)(2,1)} %param.14) | copy-start | bytes 1179652
  145.8 33.6 %copy-start.18 = (f32[1,1024]{1,0:T(1,128)S(1)}, f32[1,1024]{1,0:T(1,128)}, u32[]{:S(2)}) copy-start(f32[1,1024]{1,0:T(1,128)} %get-tuple-element.276) | copy-start | bytes 12292
  145.8 33.6 %copy-start.19 = (f32[1,1024]{1,0:T(1,128)S(1)}, f32[1,1024]{1,0:T(1,128)}, u32[]{:S(2)}) copy-start(f32[1,1024]{1,0:T(1,128)} %get-tuple-element.277) | copy-start | bytes 12292
  145.9 33.6 %copy-start.20 = (f32[1,1024]{1,0:T(1,128)S(1)}, f32[1,1024]{1,0:T(1,128)}, u32[]{:S(2)}) copy-start(f32[1,1024]{1,0:T(1,128)} %get-tuple-element.278) | copy-start | bytes 12292
  145.9 33.6 %copy-start.21 = (f32[1,1024]{1,0:T(1,128)S(1)}, f32[1,1024]{1,0:T(1,128)}, u32[]{:S(2)}) copy-start(f32[1,1024]{1,0:T(1,128)} %get-tuple-element.279) | copy-start | bytes 12292
  145.9 33.6 %copy-start.22 = (f32[1,1024]{1,0:T(1,128)S(1)}, f32[1,1024]{1,0:T(1,128)}, u32[]{:S(2)}) copy-start(f32[1,1024]{1,0:T(1,128)} %get-tuple-element.280) | copy-start | bytes 12292
  145.9 33.6 %copy-start.23 = (f32[1,1024]{1,0:T(1,128)S(1)}, f32[1,1024]{1,0:T(1,128)}, u32[]{:S(2)}) copy-start(f32[1,1024]{1,0:T(1,128)} %get-tuple-element.281) | copy-start | bytes 12292
  145.9 33.6 %copy-start.24 = (f32[1,1024]{1,0:T(1,128)S(1)}, f32[1,1024]{1,0:T(1,128)}, u32[]{:S(2)}) copy-start(f32[1,1024]{1,0:T(1,128)} %get-tuple-element.282) | copy-start | bytes 12292
  145.9 33.6 %copy-start.25 = (f32[1,1024]{1,0:T(1,128)S(1)}, f32[1,1024]{1,0:T(1,128)}, u32[]{:S(2)}) copy-start(f32[1,1024]{1,0:T(1,128)} %get-tuple-element.283) | copy-start | bytes 12292
  145.9 33.6 %copy-start.26 = (f32[1,1024]{1,0:T(1,128)S(1)}, f32[1,1024]{1,0:T(1,128)}, u32[]{:S(2)}) copy-start(f32[1,1024]{1,0:T(1,128)} %get-tuple-element.284) | copy-start | bytes 12292
  145.9 33.6 %copy-start.27 = (f32[1,1024]{1,0:T(1,128)S(1)}, f32[1,1024]{1,0:T(1,128)}, u32[]{:S(2)}) copy-start(f32[1,1024]{1,0:T(1,128)} %get-tuple-element.285) | copy-start | bytes 12292
  145.9 33.6 %copy-start.28 = (f32[1,1024]{1,0:T(1,128)S(1)}, f32[1,1024]{1,0:T(1,128)}, u32[]{:S(2)}) copy-start(f32[1,1024]{1,0:T(1,128)} %get-tuple-element.286) | copy-start | bytes 12292
  145.9 33.6 %copy-start.29 = (f32[1,1024]{1,0:T(1,128)S(1)}, f32[1,1024]{1,0:T(1,128)}, u32[]{:S(2)}) copy-start(f32[1,1024]{1,0:T(1,128)} %get-tuple-element.256) | copy-start | bytes 12292
  146.0 33.6 %copy-start.30 = (f32[1,1024]{1,0:T(1,128)S(1)}, f32[1,1024]{1,0:T(1,128)}, u32[]{:S(2)}) copy-start(f32[1,1024]{1,0:T(1,128)} %get-tuple-element.257) | copy-start | bytes 12292
  146.0 33.6 %copy-start.31 = (f32[1,1024]{1,0:T(1,128)S(1)}, f32[1,1024]{1,0:T(1,128)}, u32[]{:S(2)}) copy-start(f32[1,1024]{1,0:T(1,128)} %get-tuple-element.258) | copy-start | bytes 12292
  146.0 33.6 %copy-start.32 = (f32[1,1024]{1,0:T(1,128)S(1)}, f32[1,1024]{1,0:T(1,128)}, u32[]{:S(2)}) copy-start(f32[1,1024]{1,0:T(1,128)} %get-tuple-element.259) | copy-start | bytes 12292
  146.0 33.6 %copy-start.33 = (f32[1,1024]{1,0:T(1,128)S(1)}, f32[1,1024]{1,0:T(1,128)}, u32[]{:S(2)}) copy-start(f32[1,1024]{1,0:T(1,128)} %get-tuple-element.260) | copy-start | bytes 12292
  146.0 33.6 %copy-start.34 = (f32[1,1024]{1,0:T(1,128)S(1)}, f32[1,1024]{1,0:T(1,128)}, u32[]{:S(2)}) copy-start(f32[1,1024]{1,0:T(1,128)} %get-tuple-element.261) | copy-start | bytes 12292
  146.0 33.6 %copy-start.35 = (f32[1,1024]{1,0:T(1,128)S(1)}, f32[1,1024]{1,0:T(1,128)}, u32[]{:S(2)}) copy-start(f32[1,1024]{1,0:T(1,128)} %get-tuple-element.262) | copy-start | bytes 12292
  146.0 33.6 %copy-start.36 = (f32[1,1024]{1,0:T(1,128)S(1)}, f32[1,1024]{1,0:T(1,128)}, u32[]{:S(2)}) copy-start(f32[1,1024]{1,0:T(1,128)} %get-tuple-element.263) | copy-start | bytes 12292
  146.0 33.6 %copy-start.37 = (f32[1,1024]{1,0:T(1,128)S(1)}, f32[1,1024]{1,0:T(1,128)}, u32[]{:S(2)}) copy-start(f32[1,1024]{1,0:T(1,128)} %get-tuple-element.264) | copy-start | bytes 12292
  146.0 33.6 %copy-start.38 = (f32[1,1024]{1,0:T(1,128)S(1)}, f32[1,1024]{1,0:T(1,128)}, u32[]{:S(2)}) copy-start(f32[1,1024]{1,0:T(1,128)} %get-tuple-element.265) | copy-start | bytes 12292
  146.0 33.6 %copy-start.39 = (f32[1,1024]{1,0:T(1,128)S(1)}, f32[1,1024]{1,0:T(1,128)}, u32[]{:S(2)}) copy-start(f32[1,1024]{1,0:T(1,128)} %get-tuple-element.266) | copy-start | bytes 12292
  146.1 33.6 %copy-start.40 = (f32[1,1024]{1,0:T(1,128)S(1)}, f32[1,1024]{1,0:T(1,128)}, u32[]{:S(2)}) copy-start(f32[1,1024]{1,0:T(1,128)} %get-tuple-element.267) | copy-start | bytes 12292
  146.1 33.6 %copy-start.41 = (f32[1,1024]{1,0:T(1,128)S(1)}, f32[1,1024]{1,0:T(1,128)}, u32[]{:S(2)}) copy-start(f32[1,1024]{1,0:T(1,128)} %get-tuple-element.268) | copy-start | bytes 12292
  146.1 33.6 %copy-start.42 = (f32[1,1024]{1,0:T(1,128)S(1)}, f32[1,1024]{1,0:T(1,128)}, u32[]{:S(2)}) copy-start(f32[1,1024]{1,0:T(1,128)} %get-tuple-element.269) | copy-start | bytes 12292
  146.1 33.6 %copy-start.43 = (f32[1,1024]{1,0:T(1,128)S(1)}, f32[1,1024]{1,0:T(1,128)}, u32[]{:S(2)}) copy-start(f32[1,1024]{1,0:T(1,128)} %get-tuple-element.270) | copy-start | bytes 12292
  146.1 33.6 %copy-start.44 = (f32[1,1024]{1,0:T(1,128)S(1)}, f32[1,1024]{1,0:T(1,128)}, u32[]{:S(2)}) copy-start(f32[1,1024]{1,0:T(1,128)} %get-tuple-element.271) | copy-start | bytes 12292
  146.1 33.6 %copy-start.45 = (f32[1,1024]{1,0:T(1,128)S(1)}, f32[1,1024]{1,0:T(1,128)}, u32[]{:S(2)}) copy-start(f32[1,1024]{1,0:T(1,128)} %get-tuple-element.272) | copy-start | bytes 12292
  146.1 33.6 %copy-start.46 = (f32[1,1024]{1,0:T(1,128)S(1)}, f32[1,1024]{1,0:T(1,128)}, u32[]{:S(2)}) copy-start(f32[1,1024]{1,0:T(1,128)} %get-tuple-element.273) | copy-start | bytes 12292
  146.1 33.6 %copy-start.47 = (f32[1,1024]{1,0:T(1,128)S(1)}, f32[1,1024]{1,0:T(1,128)}, u32[]{:S(2)}) copy-start(f32[1,1024]{1,0:T(1,128)} %get-tuple-element.274) | copy-start | bytes 12292
  146.1 33.6 %copy-start.52 = (pred[192]{0:T(512)(128)(4,1)S(1)}, pred[192]{0:T(512)(128)(4,1)}, u32[]{:S(2)}) copy-start(pred[192]{0:T(512)(128)(4,1)} %get-tuple-element.287) | copy-start | bytes 580
  146.1 33.6 %copy-start.53 = (pred[192]{0:T(512)(128)(4,1)S(1)}, pred[192]{0:T(512)(128)(4,1)}, u32[]{:S(2)}) copy-start(pred[192]{0:T(512)(128)(4,1)} %get-tuple-element.288) | copy-start | bytes 580
  146.2 33.6 %copy-start.54 = (pred[192]{0:T(512)(128)(4,1)S(1)}, pred[192]{0:T(512)(128)(4,1)}, u32[]{:S(2)}) copy-start(pred[192]{0:T(512)(128)(4,1)} %get-tuple-element.289) | copy-start | bytes 580
  146.2 33.6 %copy-start.55 = (pred[192]{0:T(512)(128)(4,1)S(1)}, pred[192]{0:T(512)(128)(4,1)}, u32[]{:S(2)}) copy-start(pred[192]{0:T(512)(128)(4,1)} %get-tuple-element.290) | copy-start | bytes 580
  146.2 33.6 %copy-start.56 = (pred[192]{0:T(512)(128)(4,1)S(1)}, pred[192]{0:T(512)(128)(4,1)}, u32[]{:S(2)}) copy-start(pred[192]{0:T(512)(128)(4,1)} %get-tuple-element.291) | copy-start | bytes 580
  146.2 33.6 %copy-start.57 = (pred[192]{0:T(512)(128)(4,1)S(1)}, pred[192]{0:T(512)(128)(4,1)}, u32[]{:S(2)}) copy-start(pred[192]{0:T(512)(128)(4,1)} %get-tuple-element.292) | copy-start | bytes 580
  146.2 33.6 %copy-start.58 = (pred[192]{0:T(512)(128)(4,1)S(1)}, pred[192]{0:T(512)(128)(4,1)}, u32[]{:S(2)}) copy-start(pred[192]{0:T(512)(128)(4,1)} %get-tuple-element.293) | copy-start | bytes 580
  167.5 11.9 %collective-permute-start.1 = (bf16[30,1024]{1,0:T(8,128)(2,1)S(1)}, bf16[30,1024]{1,0:T(8,128)(2,1)S(1)}, u32[]{:S(2)}, u32[]{:S(2)}) collective-permute-start(bf16[30,1024]{1,0:T(8,128)(2,1)S(1)} %slice.1694), channel_id=1, source_target_pairs={{1,0},{2,1},{3,2},{4,3},{5,4},{6,5},{7,6},{8,7},{9,8},{10,9},{11,1... | collective-permute-start | bytes 184328 | tf_op jit(solution)/shard_map/ppermute | solution.py:15
  189.7 18.1 %copy-start.49 = (f32[1024]{0:T(1024)S(1)}, f32[1024]{0:T(1024)}, u32[]{:S(2)}) copy-start(f32[1024]{0:T(1024)} %get-tuple-element.202) | copy-start | bytes 12292
  189.7 18.1 %copy-start.50 = (f32[1024]{0:T(1024)S(1)}, f32[1024]{0:T(1024)}, u32[]{:S(2)}) copy-start(f32[1024]{0:T(1024)} %get-tuple-element.203) | copy-start | bytes 12292
  189.8 18.1 %copy-start.51 = (f32[1024]{0:T(1024)S(1)}, f32[1024]{0:T(1024)}, u32[]{:S(2)}) copy-start(f32[1024]{0:T(1024)} %get-tuple-element.204) | copy-start | bytes 12292
  193.4 22.2 %all-to-all-start.4 = ((bf16[192,16,64]{0,2,1:T(8,128)(2,1)}), bf16[192,16,64]{0,2,1:T(8,128)(2,1)}, u32[]{:S(2)}, u32[]{:S(2)}) async-start(bf16[192,16,64]{0,2,1:T(8,128)(2,1)} %bitcast.230), calls=%async_computation.4 | async-start | bytes 1048576 | tf_op jit(solution)/shard_map/all_to_all | solution.py:187
  219.0 5.8 copy-start.4
  232.8 5.8 copy-start.4
  274.1 5.8 copy-start.4
  304.4 20.5 %all-to-all-start.5 = ((bf16[16,192,64]{1,2,0:T(8,128)(2,1)}), bf16[16,192,64]{1,2,0:T(8,128)(2,1)}, u32[]{:S(2)}, u32[]{:S(2)}) async-start(bf16[16,192,64]{1,2,0:T(8,128)(2,1)} %copy.68), calls=%async_computation.5 | async-start | bytes 1048576 | tf_op jit(solution)/shard_map/all_to_all | solution.py:194
  308.7 20.4 %copy-start.6 = (f32[3072,1,64]{0,2,1:T(8,128)S(1)}, f32[3072,1,64]{0,2,1:T(8,128)}, u32[]{:S(2)}) copy-start(f32[3072,1,64]{0,2,1:T(8,128)} %get-tuple-element.117) | copy-start | bytes 2359300
  308.7 290.1 %all-reduce.3.cloned.1.call-start = ((), (), s32[]{:S(2)}) async-start(), calls=%async_computation.8 | async-start | bytes 8650752 | tf_op jit(solution)/shard_map/psum | solution.py:181
  312.6 38.7 %copy-start.3 = (bf16[192,1024]{1,0:T(8,128)(2,1)S(1)}, bf16[192,1024]{1,0:T(8,128)(2,1)}, u32[]{:S(2)}) copy-start(bf16[192,1024]{1,0:T(8,128)(2,1)} %copy-done.1) | copy-start | bytes 1179652
  324.8 22.7 %all-to-all-start.6 = ((bf16[16,192,64]{1,2,0:T(8,128)(2,1)}), bf16[16,192,64]{1,2,0:T(8,128)(2,1)}, u32[]{:S(2)}, u32[]{:S(2)}) async-start(bf16[16,192,64]{1,2,0:T(8,128)(2,1)} %copy.69), calls=%async_computation.6 | async-start | bytes 1048576 | tf_op jit(solution)/shard_map/all_to_all | solution.py:195
  347.5 21.7 %all-to-all-start.7 = ((bf16[16,192,64]{1,2,0:T(8,128)(2,1)}), bf16[16,192,64]{1,2,0:T(8,128)(2,1)S(1)}, u32[]{:S(2)}, u32[]{:S(2)}) async-start(bf16[16,192,64]{1,2,0:T(8,128)(2,1)} %copy.70), calls=%async_computation.7 | async-start | bytes 1048576 | tf_op jit(solution)/shard_map/all_to_all | solution.py:196
  (31 other events, 112.3 us)
Sparse Core Ops, SparseCore 0:
  315.6 283.1 all-reduce.2
where the time goes:
time: 615 us; the launch traced here: 611 us
  waiting for transfers between devices  314 us (51%)
  matrix products  84.2 us (14%)
  other arithmetic  76 us (12%)
  local copies, waits for them, and re-layouts  68.6 us (11%)
  starting transfers between devices  44.5 us (7%)
  between operations  15 us (2%)
  loops' own time  8.71 us (1%)
    psum x1, waiting for transfers between devices, local(): summed = lax.psum((weight_local, conv_local), ('dp', 'seq'))  229 us
    reduce_sum x6, other arithmetic, tap_sums(): rows_out.append(jnp.sum(jnp.where(same, signal * window, 0.0), axis=0))  38.3 us
    dot_general x12, matrix products, block_scores(): jnp.einsum('qhd,khd->hqk', query_blk, key_part, preferred_element_type=jn...  28.9 us
    all_to_all x1, waiting for transfers between devices, local(): lax.all_to_all(grad_k.reshape(total, -1), 'seq', split_axis=0, concat_axi...  15 us
    all_to_all x1, waiting for transfers between devices, local(): lax.all_to_all(key_proj[0], 'seq', split_axis=1, concat_axis=0, tiled=True)  14.6 us
    unnamed x114, local copies, waits for them, and re-layouts  12.8 us
  transfers between devices with their start and end apart: 11, of which 9 were waited for; matrix products, arithmetic and copies ran while one was open for 9% of the time, Pallas kernels for 0%

commit v1 on v0

--- a/solution.py
+++ b/solution.py
@@ -178,7 +178,7 @@
     weight_local = lax.dot_general(
         mixed_rows, proj_back, (((0,), (0,)), ((), ())), preferred_element_type=jnp.float32
     )
-    summed = lax.psum((weight_local, conv_local), ("dp", "seq"))
+    summed = lax.psum(lax.psum((weight_local, conv_local), "dp"), "seq")
     weight_grad = summed[0] * factor
     conv_grad = summed[1] * factor
     mixed_back = lax.dot_general(

time: 615 us -> 494 us (0.80)
  waiting for transfers between devices: 314 us -> 184 us
  local copies, waits for them, and re-layouts: 68.6 us -> 75.4 us
  starting transfers between devices: 44.5 us -> 50.7 us
    psum x1 -> x2, waiting for transfers between devices: 229 us -> 104 us  [local(): summed = lax.psum(lax.psum((weight_local, conv_local), 'dp'), 'seq')]
    unnamed x114 -> x66, local copies, waits for them, and re-layouts: 12.8 us -> 12.7 us
  transfers between devices with their start and end apart: 11 -> 12, of which waited for: 9 -> 9; matrix products, arithmetic and copies ran while one was open for 9% -> 27% of each run, Pallas kernels for 0% -> 0%
where the time goes in v1:
time: 494 us; the launch traced here: 490 us
  waiting for transfers between devices  184 us (37%)
  matrix products  83.5 us (17%)
  local copies, waits for them, and re-layouts  75.4 us (15%)
  other arithmetic  73.9 us (15%)
  starting transfers between devices  50.7 us (10%)
  between operations  14.6 us (3%)
  loops' own time  8.09 us (2%)
    psum x2, waiting for transfers between devices, local(): summed = lax.psum(lax.psum((weight_local, conv_local), 'dp'), 'seq')  104 us
    reduce_sum x6, other arithmetic, tap_sums(): rows_out.append(jnp.sum(jnp.where(same, signal * window, 0.0), axis=0))  37.2 us
    dot_general x12, matrix products, block_scores(): jnp.einsum('qhd,khd->hqk', query_blk, key_part, preferred_element_type=jn...  28.9 us
    all_to_all x1, waiting for transfers between devices, local(): lax.all_to_all(key_proj[0], 'seq', split_axis=1, concat_axis=0, tiled=True)  15.9 us
    all_to_all x1, waiting for transfers between devices, local(): lax.all_to_all(grad_k.reshape(total, -1), 'seq', split_axis=0, concat_axi...  15.1 us
    all_to_all x1, waiting for transfers between devices, local(): lax.all_to_all(mixed_heads.reshape(total, -1), 'seq', split_axis=0, conca...  13.4 us
    unnamed x66, local copies, waits for them, and re-layouts  12.7 us
    all_to_all x1, waiting for transfers between devices, local(): lax.all_to_all(grad_v.reshape(total, -1), 'seq', split_axis=0, concat_axi...  12 us
  transfers between devices with their start and end apart: 12, of which 9 were waited for; matrix products, arithmetic and copies ran while one was open for 27% of the time, Pallas kernels for 0%

profile of v1, /device:TPU:2, one launch (start us, length us, event | category | flops | bytes accessed | tf_op | source)
XLA Modules:
  0.0 490.5 jit_solution(7153374393755855353)
XLA Ops:
  7.2 2.1 copy.56
  9.3 8.6 %all-to-all-start = ((bf16[192,16,64]{0,2,1:T(8,128)(2,1)}), bf16[192,16,64]{0,2,1:T(8,128)(2,1)S(1)}, u32[]{:S(2)}, u32[]{:S(2)}) async-start(bf16[192,16,64]{0,2,1:T(8,128)(2,1)} %bitcast.10), calls=%async_computation | async-start | bytes 1048576 | tf_op jit(solution)/shard_map/all_to_all | solution.py:143
  17.9 2.0 copy.58
  19.9 2.0 copy.60
  21.9 12.0 %all-to-all-done = bf16[192,16,64]{0,2,1:T(8,128)(2,1)S(1)} async-done(((bf16[192,16,64]{0,2,1:T(8,128)(2,1)}), bf16[192,16,64]{0,2,1:T(8,128)(2,1)S(1)}, u32[]{:S(2)}, u32[]{:S(2)}) %all-to-all-start) | async-done | bytes 393248 | tf_op jit(solution)/shard_map/all_to_all | solution.py:143
  33.9 4.2 all-to-all-start.1
  38.4 15.9 %all-to-all-done.1 = bf16[192,16,64]{0,2,1:T(8,128)(2,1)S(1)} async-done(((bf16[192,16,64]{0,2,1:T(8,128)(2,1)}), bf16[192,16,64]{0,2,1:T(8,128)(2,1)S(1)}, u32[]{:S(2)}, u32[]{:S(2)}) %all-to-all-start.1) | async-done | bytes 393248 | tf_op jit(solution)/shard_map/all_to_all | solution.py:144
  54.3 4.2 all-to-all-start.2
  64.1 10.5 %all-to-all-done.2 = bf16[192,16,64]{0,2,1:T(8,128)(2,1)} async-done(((bf16[192,16,64]{0,2,1:T(8,128)(2,1)}), bf16[192,16,64]{0,2,1:T(8,128)(2,1)}, u32[]{:S(2)}, u32[]{:S(2)}) %all-to-all-start.2) | async-done | bytes 393248 | tf_op jit(solution)/shard_map/all_to_all | solution.py:145
  76.6 41.2 %while.27 = (s32[]{:T(128)}, bf16[6,512,1,64]{1,3,2,0:T(8,128)(2,1)S(1)}, f32[6,1,512]{2,1,0:T(1,128)}, s32[6]{0:T(128)S(1)}, s32[3072]{0:T(1024)}, /*index=5*/b...) while((s32[]{:T(128)}, ...), condition=%wide.region_4.5_spmd, body=%wide.region_1.4_spmd.sunk | while | flops 415268352 | bytes 19828936 | solution.py:94
  78.6 2.1 fusion.340
  85.5 2.1 fusion.340
  92.3 2.1 fusion.340
  99.2 2.1 fusion.340
  106.0 2.1 fusion.340
  112.9 2.1 fusion.340
  118.8 2.5 all_to_all.107
  121.3 2.0 copy.63
  123.3 4.1 all-to-all-start.3
  130.2 13.4 %all-to-all-done.3 = bf16[16,192,64]{1,2,0:T(8,128)(2,1)S(1)} async-done(((bf16[16,192,64]{1,2,0:T(8,128)(2,1)}), bf16[16,192,64]{1,2,0:T(8,128)(2,1)S(1)}, u32[]{:S(2)}, u32[]{:S(2)}) %all-to-all-start.3) | async-done | bytes 393248 | tf_op jit(solution)/shard_map/all_to_all | solution.py:152
  145.0 3.6 collective-permute-start
  152.0 19.7 %fusion.155 = (f32[1024]{0:T(1024)S(1)}, f32[192,1024]{1,0:T(8,128)S(1)}, f32[192,1024]{1,0:T(8,128)}) fusion(bf16[192,1024]{1,0:T(8,128)(2,1)} %copy-done.1, pred[192]{0:T(512)(128)(4,1)} %get-tuple-element.320, bf16[1,192,1024]{2,1,0:T(8,128)(2,1)} %param.14, f32[1024]{0:T(1024)} %bitcast.257, bf16[30,1024]{1,0:T(8,128)(2,1)S(1)} %collective-permute-done, ...), kind=kLoop, calls=%fused_computation.322 | loop fusion | flops 44235776 | bytes 2557760 | tf_op jit(solution)/shard_map/reduce_sum | solution.py:51
  173.0 4.1 fusion.90
  177.2 2.1 fusion.108
  179.3 2.7 fusion.72
  182.1 9.5 %fusion.151 = bf16[192,1024]{1,0:T(8,128)(2,1)S(1)} fusion(f32[192,1024]{1,0:T(8,128)S(1)} %get-tuple-element.252, f32[30,1024]{1,0:T(8,128)S(1)} %convert_element_type.251, bf16[1,192,1024]{2,1,0:T(8,128)(2,1)S(1)} %copy-done.13, f32[1024]{0:T(1024)} %bitcast.258, f32[1024]{0:T(1024)} %bitcast.260, f32[1024]{0:T(1024)} %bitcast.264, f32[1024]{0:T(1024)} %bitcast.266, ...), kind=kLoop, calls=%fused_computation.318 | loop fusion | flops 24576000 | bytes 1828672 | tf_op jit(solution)/shard_map/convert_element_type | solution.py:175
  194.0 2.0 copy.64
  196.0 6.2 %all-to-all-start.4 = ((bf16[192,16,64]{0,2,1:T(8,128)(2,1)}), bf16[192,16,64]{0,2,1:T(8,128)(2,1)}, u32[]{:S(2)}, u32[]{:S(2)}) async-start(bf16[192,16,64]{0,2,1:T(8,128)(2,1)} %bitcast.230), calls=%async_computation.4 | async-start | bytes 1048576 | tf_op jit(solution)/shard_map/all_to_all | solution.py:187
  202.5 4.2 fusion.126
  206.7 4.2 fusion.150
  211.0 2.7 stack.127
  213.6 3.9 fusion.313
  218.3 2.1 copy.65
  220.4 2.4 reshape.262
  223.6 80.9 %while.28 = (s32[]{:T(128)}, f32[3072,1,64]{0,2,1:T(8,128)}, f32[3072,1,64]{0,2,1:T(8,128)S(1)}, bf16[6,512,1,64]{1,3,2,0:T(8,128)(2,1)}, s32[6]{0:T(128)S(1)}, ...) while((s32[]{:T(128)}, f32[3072,1,64]{0,2,1:T(8,128)}, ...), condition=%wide.region_10.11_spmd.clone, body=%wide.region_8.10_spmd.clone.sunk | while | flops 1021967872 | bytes 31551828 | solution.py:127
  226.5 2.7 exponential_convert_fusion.12
  231.0 2.0 multiply_convert_fusion.2
  240.0 2.7 exponential_convert_fusion.12
  244.4 2.0 multiply_convert_fusion.2
  253.5 2.7 exponential_convert_fusion.12
  257.9 2.0 multiply_convert_fusion.2
  267.0 2.7 exponential_convert_fusion.12
  271.4 2.0 multiply_convert_fusion.2
  280.5 2.7 exponential_convert_fusion.12
  284.8 2.0 multiply_convert_fusion.2
  293.9 2.7 exponential_convert_fusion.12
  298.3 2.0 multiply_convert_fusion.2
  304.5 2.0 copy.67
  306.5 2.5 all_to_all.114
  309.0 2.0 copy.68
  311.0 6.5 %all-to-all-start.5 = ((bf16[16,192,64]{1,2,0:T(8,128)(2,1)}), bf16[16,192,64]{1,2,0:T(8,128)(2,1)}, u32[]{:S(2)}, u32[]{:S(2)}) async-start(bf16[16,192,64]{1,2,0:T(8,128)(2,1)} %copy.68), calls=%async_computation.5 | async-start | bytes 1048576 | tf_op jit(solution)/shard_map/all_to_all | solution.py:194
  317.6 16.7 %all-reduce.7.cloned.1.call-done = (f32[1024,1024]{1,0:T(8,128)}, f32[31,1024]{1,0:T(8,128)}) async-done(((f32[1024,1024]{1,0:T(8,128)}, f32[31,1024]{1,0:T(8,128)}), (f32[1024,1024]{1,0:T(8,128)}, f32[31,1024]{1,0:T(8,128)})) %all-reduce.7.cloned.1.call-update) | async-done | bytes 4321296 | tf_op jit(solution)/shard_map/psum | solution.py:181
  334.3 2.0 convert_element_type.254
  336.3 2.4 all_to_all.117
  338.7 2.0 copy.69
  340.7 7.2 %all-to-all-start.6 = ((bf16[16,192,64]{1,2,0:T(8,128)(2,1)}), bf16[16,192,64]{1,2,0:T(8,128)(2,1)}, u32[]{:S(2)}, u32[]{:S(2)}) async-start(bf16[16,192,64]{1,2,0:T(8,128)(2,1)} %copy.69), calls=%async_computation.6 | async-start | bytes 1048576 | tf_op jit(solution)/shard_map/all_to_all | solution.py:195
  351.3 15.1 %all-to-all-done.6 = bf16[16,192,64]{1,2,0:T(8,128)(2,1)} async-done(((bf16[16,192,64]{1,2,0:T(8,128)(2,1)}), bf16[16,192,64]{1,2,0:T(8,128)(2,1)}, u32[]{:S(2)}, u32[]{:S(2)}) %all-to-all-start.6) | async-done | bytes 393248 | tf_op jit(solution)/shard_map/all_to_all | solution.py:195
  366.4 4.6 all-to-all-start.7
  371.0 2.1 fusion.304
  373.1 2.0 copy.71
  375.1 2.0 copy.72
  377.1 12.0 %all-to-all-done.7 = bf16[16,192,64]{1,2,0:T(8,128)(2,1)S(1)} async-done(((bf16[16,192,64]{1,2,0:T(8,128)(2,1)}), bf16[16,192,64]{1,2,0:T(8,128)(2,1)S(1)}, u32[]{:S(2)}, u32[]{:S(2)}) %all-to-all-start.7) | async-done | bytes 393248 | tf_op jit(solution)/shard_map/all_to_all | solution.py:196
  390.1 87.8 %all-reduce.5.cloned.1.call-done = (f32[1024,1024]{1,0:T(8,128)}, f32[31,1024]{1,0:T(8,128)}) async-done(((f32[1024,1024]{1,0:T(8,128)}, f32[31,1024]{1,0:T(8,128)}), (f32[1024,1024]{1,0:T(8,128)}, f32[31,1024]{1,0:T(8,128)})) %all-reduce.5.cloned.1.call-update) | async-done | bytes 4321296 | tf_op jit(solution)/shard_map/psum | solution.py:181
  477.8 5.2 %broadcast_multiply_fusion = f32[1024,1024]{1,0:T(8,128)} fusion(f32[1024,1024]{1,0:T(8,128)} %get-tuple-element.247), kind=kLoop, calls=%fused_computation.101 | loop fusion | flops 1048576 | bytes 8388608 | tf_op jit(solution)/shard_map/mul | solution.py:182
  (223 shorter events, 100.0 us)
Async XLA Ops:
  7.2 136.4 %copy-start = (bf16[1024,1024]{1,0:T(8,128)(2,1)S(1)}, bf16[1024,1024]{1,0:T(8,128)(2,1)}, u32[]{:S(2)}) copy-start(bf16[1024,1024]{1,0:T(8,128)(2,1)} %param.15) | copy-start | bytes 6291460
  7.2 31.0 %copy-start.20 = (s32[1,2]{1,0:T(1,128)S(1)}, s32[1,2]{1,0:T(1,128)}, u32[]{:S(2)}) copy-start(s32[1,2]{1,0:T(1,128)} %param.17) | copy-start | bytes 28
  9.3 24.6 %all-to-all-start = ((bf16[192,16,64]{0,2,1:T(8,128)(2,1)}), bf16[192,16,64]{0,2,1:T(8,128)(2,1)S(1)}, u32[]{:S(2)}, u32[]{:S(2)}) async-start(bf16[192,16,64]{0,2,1:T(8,128)(2,1)} %bitcast.10), calls=%async_computation | async-start | bytes 1048576 | tf_op jit(solution)/shard_map/all_to_all | solution.py:143
  33.9 20.4 %all-to-all-start.1 = ((bf16[192,16,64]{0,2,1:T(8,128)(2,1)}), bf16[192,16,64]{0,2,1:T(8,128)(2,1)S(1)}, u32[]{:S(2)}, u32[]{:S(2)}) async-start(bf16[192,16,64]{0,2,1:T(8,128)(2,1)} %bitcast.12), calls=%async_computation.1 | async-start | bytes 1048576 | tf_op jit(solution)/shard_map/all_to_all | solution.py:144
  54.3 6.3 %copy-start.12 = (bf16[192,16,64]{0,2,1:T(8,128)(2,1)}, bf16[192,16,64]{0,2,1:T(8,128)(2,1)S(1)}, u32[]{:S(2)}) copy-start(bf16[192,16,64]{0,2,1:T(8,128)(2,1)S(1)} %all-to-all-done.1) | copy-start | bytes 1179652
  54.3 20.3 %all-to-all-start.2 = ((bf16[192,16,64]{0,2,1:T(8,128)(2,1)}), bf16[192,16,64]{0,2,1:T(8,128)(2,1)}, u32[]{:S(2)}, u32[]{:S(2)}) async-start(bf16[192,16,64]{0,2,1:T(8,128)(2,1)} %bitcast.14), calls=%async_computation.2 | async-start | bytes 1048576 | tf_op jit(solution)/shard_map/all_to_all | solution.py:145
  59.3 68.9 %copy-start.17 = (s32[192]{0:T(256)}, s32[192]{0:T(256)S(1)}, u32[]{:S(2)}) copy-start(s32[192]{0:T(256)S(1)} %get-tuple-element.255) | copy-start | bytes 2308
  76.6 52.3 %copy-start.15 = (f32[31,1024]{1,0:T(8,128)S(1)}, f32[31,1024]{1,0:T(8,128)}, u32[]{:S(2)}) copy-start(f32[31,1024]{1,0:T(8,128)} %param.16) | copy-start | bytes 380932
  117.8 5.5 %copy-start.10 = (bf16[6,512,1,64]{1,3,2,0:T(8,128)(2,1)}, bf16[6,512,1,64]{1,3,2,0:T(8,128)(2,1)S(1)}, u32[]{:S(2)}) copy-start(bf16[6,512,1,64]{1,3,2,0:T(8,128)(2,1)S(1)} %get-tuple-element.113) | copy-start | bytes 1179652
  117.8 34.2 %copy-start.7 = (bf16[3072,1,64]{0,2,1:T(8,128)(2,1)}, bf16[3072,1,64]{0,2,1:T(8,128)(2,1)S(1)}, u32[]{:S(2)}) copy-start(bf16[3072,1,64]{0,2,1:T(8,128)(2,1)S(1)} %get-tuple-element.573) | copy-start | bytes 1179652
  123.3 20.3 %all-to-all-start.3 = ((bf16[16,192,64]{1,2,0:T(8,128)(2,1)}), bf16[16,192,64]{1,2,0:T(8,128)(2,1)S(1)}, u32[]{:S(2)}, u32[]{:S(2)}) async-start(bf16[16,192,64]{1,2,0:T(8,128)(2,1)} %copy.63), calls=%async_computation.3 | async-start | bytes 1048576 | tf_op jit(solution)/shard_map/all_to_all | solution.py:152
  143.6 8.4 %copy-start.9 = (bf16[16,192,64]{1,2,0:T(8,128)(2,1)}, bf16[16,192,64]{1,2,0:T(8,128)(2,1)S(1)}, u32[]{:S(2)}) copy-start(bf16[16,192,64]{1,2,0:T(8,128)(2,1)S(1)} %all-to-all-done.3) | copy-start | bytes 1179652
  144.2 0.7 copy-start.1
  145.0 7.0 %collective-permute-start = (bf16[30,1024]{1,0:T(8,128)(2,1)S(1)}, bf16[30,1024]{1,0:T(8,128)(2,1)S(1)}, u32[]{:S(2)}, u32[]{:S(2)}) collective-permute-start(bf16[30,1024]{1,0:T(8,128)(2,1)S(1)} %slice.713), channel_id=1, source_target_pairs={{0,1},{1,2},{2,3},{3,4},{4,5},{5,6},{6,7},{7,8},{8,9},{9,10},{10,1... | collective-permute-start | bytes 184328 | tf_op jit(solution)/shard_map/ppermute | solution.py:15
  150.0 27.3 %copy-start.2 = (bf16[192,1024]{1,0:T(8,128)(2,1)S(1)}, bf16[192,1024]{1,0:T(8,128)(2,1)}, u32[]{:S(2)}) copy-start(bf16[192,1024]{1,0:T(8,128)(2,1)} %copy-done.1) | copy-start | bytes 1179652
  150.0 32.1 %copy-start.13 = (bf16[1,192,1024]{2,1,0:T(8,128)(2,1)S(1)}, bf16[1,192,1024]{2,1,0:T(8,128)(2,1)}, u32[]{:S(2)}) copy-start(bf16[1,192,1024]{2,1,0:T(8,128)(2,1)} %param.14) | copy-start | bytes 1179652
  150.0 32.0 %copy-start.21 = (pred[192]{0:T(512)(128)(4,1)S(1)}, pred[192]{0:T(512)(128)(4,1)}, u32[]{:S(2)}) copy-start(pred[192]{0:T(512)(128)(4,1)} %get-tuple-element.307) | copy-start | bytes 580
  150.0 32.0 %copy-start.22 = (pred[192]{0:T(512)(128)(4,1)S(1)}, pred[192]{0:T(512)(128)(4,1)}, u32[]{:S(2)}) copy-start(pred[192]{0:T(512)(128)(4,1)} %get-tuple-element.308) | copy-start | bytes 580
  150.0 32.0 %copy-start.23 = (pred[192]{0:T(512)(128)(4,1)S(1)}, pred[192]{0:T(512)(128)(4,1)}, u32[]{:S(2)}) copy-start(pred[192]{0:T(512)(128)(4,1)} %get-tuple-element.309) | copy-start | bytes 580
  150.0 32.0 %copy-start.24 = (pred[192]{0:T(512)(128)(4,1)S(1)}, pred[192]{0:T(512)(128)(4,1)}, u32[]{:S(2)}) copy-start(pred[192]{0:T(512)(128)(4,1)} %get-tuple-element.310) | copy-start | bytes 580
  150.0 32.0 %copy-start.25 = (pred[192]{0:T(512)(128)(4,1)S(1)}, pred[192]{0:T(512)(128)(4,1)}, u32[]{:S(2)}) copy-start(pred[192]{0:T(512)(128)(4,1)} %get-tuple-element.311) | copy-start | bytes 580
  150.0 32.0 %copy-start.26 = (pred[192]{0:T(512)(128)(4,1)S(1)}, pred[192]{0:T(512)(128)(4,1)}, u32[]{:S(2)}) copy-start(pred[192]{0:T(512)(128)(4,1)} %get-tuple-element.312) | copy-start | bytes 580
  150.0 32.0 %copy-start.27 = (pred[192]{0:T(512)(128)(4,1)S(1)}, pred[192]{0:T(512)(128)(4,1)}, u32[]{:S(2)}) copy-start(pred[192]{0:T(512)(128)(4,1)} %get-tuple-element.313) | copy-start | bytes 580
  150.0 32.0 %copy-start.28 = (pred[192]{0:T(512)(128)(4,1)S(1)}, pred[192]{0:T(512)(128)(4,1)}, u32[]{:S(2)}) copy-start(pred[192]{0:T(512)(128)(4,1)} %get-tuple-element.314) | copy-start | bytes 580
  150.1 32.0 %copy-start.29 = (pred[192]{0:T(512)(128)(4,1)S(1)}, pred[192]{0:T(512)(128)(4,1)}, u32[]{:S(2)}) copy-start(pred[192]{0:T(512)(128)(4,1)} %get-tuple-element.315) | copy-start | bytes 580
  150.1 32.0 %copy-start.30 = (pred[192]{0:T(512)(128)(4,1)S(1)}, pred[192]{0:T(512)(128)(4,1)}, u32[]{:S(2)}) copy-start(pred[192]{0:T(512)(128)(4,1)} %get-tuple-element.316) | copy-start | bytes 580
  150.1 32.0 %copy-start.31 = (pred[192]{0:T(512)(128)(4,1)S(1)}, pred[192]{0:T(512)(128)(4,1)}, u32[]{:S(2)}) copy-start(pred[192]{0:T(512)(128)(4,1)} %get-tuple-element.317) | copy-start | bytes 580
  150.1 32.0 %copy-start.32 = (pred[192]{0:T(512)(128)(4,1)S(1)}, pred[192]{0:T(512)(128)(4,1)}, u32[]{:S(2)}) copy-start(pred[192]{0:T(512)(128)(4,1)} %get-tuple-element.318) | copy-start | bytes 580
  171.7 10.3 %collective-permute-start.1 = (bf16[30,1024]{1,0:T(8,128)(2,1)S(1)}, bf16[30,1024]{1,0:T(8,128)(2,1)S(1)}, u32[]{:S(2)}, u32[]{:S(2)}) collective-permute-start(bf16[30,1024]{1,0:T(8,128)(2,1)S(1)} %slice.1694), channel_id=1, source_target_pairs={{1,0},{2,1},{3,2},{4,3},{5,4},{6,5},{7,6},{8,7},{9,8},{10,9},{11,1... | collective-permute-start | bytes 184328 | tf_op jit(solution)/shard_map/ppermute | solution.py:15
  191.6 0.8 copy-start.11
  192.4 18.6 %copy-start.18 = (f32[1024]{0:T(1024)S(1)}, f32[1024]{0:T(1024)}, u32[]{:S(2)}) copy-start(f32[1024]{0:T(1024)} %get-tuple-element.203) | copy-start | bytes 12292
  192.4 18.6 %copy-start.19 = (f32[1024]{0:T(1024)S(1)}, f32[1024]{0:T(1024)}, u32[]{:S(2)}) copy-start(f32[1024]{0:T(1024)} %get-tuple-element.204) | copy-start | bytes 12292
  196.0 22.2 %all-to-all-start.4 = ((bf16[192,16,64]{0,2,1:T(8,128)(2,1)}), bf16[192,16,64]{0,2,1:T(8,128)(2,1)}, u32[]{:S(2)}, u32[]{:S(2)}) async-start(bf16[192,16,64]{0,2,1:T(8,128)(2,1)} %bitcast.230), calls=%async_computation.4 | async-start | bytes 1048576 | tf_op jit(solution)/shard_map/all_to_all | solution.py:187
  202.2 132.1 %all-reduce.7.cloned.1.call-start = ((), (), s32[]{:S(2)}) async-start(), calls=%async_computation.9 | async-start | bytes 8650752 | tf_op jit(solution)/shard_map/psum | solution.py:181
  217.5 6.1 %copy-start.4 = (f32[3072,1,64]{0,2,1:T(8,128)S(1)}, f32[3072,1,64]{0,2,1:T(8,128)}, u32[]{:S(2)}) copy-start(f32[3072,1,64]{0,2,1:T(8,128)} %custom-call.1) | copy-start | bytes 2359300
  217.5 6.1 %copy-start.16 = (s32[3072]{0:T(1024)S(1)}, s32[3072]{0:T(1024)}, u32[]{:S(2)}) copy-start(s32[3072]{0:T(1024)} %get-tuple-element.598) | copy-start | bytes 36868
  230.9 2.0 copy-start.8
  230.9 3.7 copy-start.5
  236.2 0.9 copy-start.6
  244.4 2.0 copy-start.8
  244.4 3.7 copy-start.5
  249.7 0.9 copy-start.6
  257.9 2.0 copy-start.8
  257.9 3.7 copy-start.5
  263.2 0.9 copy-start.6
  271.4 2.0 copy-start.8
  271.4 3.7 copy-start.5
  276.7 0.9 copy-start.6
  284.8 2.0 copy-start.8
  284.8 3.7 copy-start.5
  290.1 0.9 copy-start.6
  298.3 2.0 copy-start.8
  298.3 3.7 copy-start.5
  303.6 0.9 copy-start.6
  311.0 29.7 %all-to-all-start.5 = ((bf16[16,192,64]{1,2,0:T(8,128)(2,1)}), bf16[16,192,64]{1,2,0:T(8,128)(2,1)}, u32[]{:S(2)}, u32[]{:S(2)}) async-start(bf16[16,192,64]{1,2,0:T(8,128)(2,1)} %copy.68), calls=%async_computation.5 | async-start | bytes 1048576 | tf_op jit(solution)/shard_map/all_to_all | solution.py:194
  317.5 160.3 %all-reduce.5.cloned.1.call-start = ((), (), s32[]{:S(2)}) async-start(), calls=%async_computation.8 | async-start | bytes 8650752 | tf_op jit(solution)/shard_map/psum | solution.py:181
  334.3 36.7 %copy-start.3 = (bf16[192,1024]{1,0:T(8,128)(2,1)S(1)}, bf16[192,1024]{1,0:T(8,128)(2,1)}, u32[]{:S(2)}) copy-start(bf16[192,1024]{1,0:T(8,128)(2,1)} %copy-done.1) | copy-start | bytes 1179652
  340.7 25.6 %all-to-all-start.6 = ((bf16[16,192,64]{1,2,0:T(8,128)(2,1)}), bf16[16,192,64]{1,2,0:T(8,128)(2,1)}, u32[]{:S(2)}, u32[]{:S(2)}) async-start(bf16[16,192,64]{1,2,0:T(8,128)(2,1)} %copy.69), calls=%async_computation.6 | async-start | bytes 1048576 | tf_op jit(solution)/shard_map/all_to_all | solution.py:195
  366.4 22.7 %all-to-all-start.7 = ((bf16[16,192,64]{1,2,0:T(8,128)(2,1)}), bf16[16,192,64]{1,2,0:T(8,128)(2,1)S(1)}, u32[]{:S(2)}, u32[]{:S(2)}) async-start(bf16[16,192,64]{1,2,0:T(8,128)(2,1)} %copy.70), calls=%async_computation.7 | async-start | bytes 1048576 | tf_op jit(solution)/shard_map/all_to_all | solution.py:196
  477.8 5.2 %copy-start.14 = (f32[31,1024]{1,0:T(8,128)S(1)}, f32[31,1024]{1,0:T(8,128)}, u32[]{:S(2)}) copy-start(f32[31,1024]{1,0:T(8,128)} %get-tuple-element.248) | copy-start | bytes 380932
Sparse Core Ops, SparseCore 0:
  217.7 116.5 all-reduce.6
  336.9 140.8 all-reduce.4
